TPU v7x, 32 devices: a whole 2x2x4 slice. The times are simulated.
32 devices in a mesh: groups: 2 (over x), row: 16 (over z, y, core).
Axes of the slice: x: 2, y: 2, z: 4, core: 2. Of those that a mesh axis runs over, the one named last changes fastest.
Arguments:
- orbitals: bfloat16 [4096, 512], P(('groups', 'row')), parts along dimension 0, may hold values from -1.296875 to 1.296875
- basis: bfloat16 [4096, 1024], P(('groups', 'row')), parts along dimension 0, may hold values from -0.1875 to 0.1875
- kernel: bfloat16 [4096, 2048], P(('groups', 'row')), parts along dimension 0, may hold values from -6 to 6
Outputs:
- exchange_matrix: float32 [2048, 1024], P('groups', 'row'), parts along dimension 0
There are 2 independent parts, one for each index of `groups`. A program takes and returns all parts, laid end to end along the dimension named above; each array names one. Nothing has to cross between parts.
All inputs are finite; a program needn't handle non-finite values.
Results may differ from a plain program's by a relative error of at most 0.0041.
Values may be sent and summed in bfloat16 or wider, within the bound.
A program may use at most 128 MiB of HBM per device.

v0:
```python
import jax
import jax.numpy as jnp
from jax import lax
from jax.sharding import PartitionSpec as P


def shards(orbitals, basis, kernel):
    density = lax.dot_general(
        orbitals,
        lax.all_gather(orbitals, "row", axis=0, tiled=True),
        (((1,), (1,)), ((), ())),
        preferred_element_type=jnp.float32,
    )
    weighted = (density * kernel.astype(jnp.float32)).astype(jnp.bfloat16)
    whole_basis = lax.all_gather(basis, "row", axis=0, tiled=True)
    applied = jnp.dot(weighted, whole_basis, preferred_element_type=jnp.float32).astype(
        jnp.bfloat16
    )
    received = lax.all_to_all(applied, "row", split_axis=1, concat_axis=0, tiled=True)
    exchange_matrix = lax.dot_general(
        whole_basis, received, (((0,), (0,)), ((), ())), preferred_element_type=jnp.float32
    )
    return exchange_matrix


def solution(mesh):
    return jax.shard_map(
        shards,
        mesh=mesh,
        in_specs=(
            P(("groups", "row"), None),
            P(("groups", "row"), None),
            P(("groups", "row"), None),
        ),
        out_specs=P("groups", "row"),
        check_vma=False,
    )
```

profile of v0, /device:TPU:0, one launch (start us, length us, event | category | flops | bytes accessed | tf_op | source)
XLA Modules:
  0.0 133.2 jit_solution(10812226006285130068)
XLA Ops:
  6.5 0.0 all-gather.3.cloned.1.call-start
  6.5 0.7 all-gather.3.cloned.1.call-update
  7.3 0.0 all-gather.5.cloned.1.call-start
  7.3 0.7 all-gather.5.cloned.1.call-update
  8.0 45.7 %all-gather.3.cloned.1.call-done = bf16[2048,512]{1,0:T(8,128)(2,1)} async-done(((bf16[128,512]{1,0:T(8,128)(2,1)}), bf16[2048,512]{1,0:T(8,128)(2,1)}) %all-gather.3.cloned.1.call-update) | async-done | bytes 2097168 | tf_op jit(solution)/shard_map/all_gather | solution.py:10
  53.7 51.3 %all-gather.5.cloned.1.call-done = bf16[2048,1024]{1,0:T(8,128)(2,1)} async-done(((bf16[128,1024]{1,0:T(8,128)(2,1)}), bf16[2048,1024]{1,0:T(8,128)(2,1)}) %all-gather.5.cloned.1.call-update) | async-done | bytes 4194320 | tf_op jit(solution)/shard_map/all_gather | solution.py:15
  105.0 4.4 %convolution_convert_fusion = bf16[128,1024]{1,0:T(8,128)(2,1)S(1)} fusion(bf16[2048,1024]{1,0:T(8,128)(2,1)} %all-gather.5.cloned.1.call-done, bf16[128,512]{1,0:T(8,128)(2,1)} %param.3, bf16[2048,512]{1,0:T(8,128)(2,1)} %all-gather.3.cloned.1.call-done, bf16[128,2048]{1,0:T(8,128)(2,1)} %param.5), kind=kOutput, calls=%fused_computation.2 | convolution fusion | flops 806223872 | bytes 7208960 | tf_op jit(solution)/shard_map/dot_general | solution.py:16
  109.4 0.2 copy.4
  109.6 13.1 %all_to_all.19 = bf16[128,16,64]{0,2,1:T(8,128)(2,1)S(1)} all-to-all(bf16[128,16,64]{0,2,1:T(8,128)(2,1)S(1)} %bitcast.15), channel_id=1, replica_groups=mesh['groups'=2,'row'=16] {'row'}, dimensions={1} | all-to-all | bytes 524288 | tf_op jit(solution)/shard_map/all_to_all | solution.py:19
  122.6 3.7 %convolution_bitcast_fusion = f32[1024,64]{0,1:T(8,128)} fusion(bf16[2048,1024]{1,0:T(8,128)(2,1)} %all-gather.5.cloned.1.call-done, bf16[128,16,64]{0,2,1:T(8,128)(2,1)S(1)} %all_to_all.19), kind=kOutput, calls=%fused_computation.3 | convolution fusion | flops 268435456 | bytes 4718592 | tf_op jit(solution)/shard_map/dot_general | solution.py:20
Async XLA Ops:
  6.5 47.2 %all-gather.3.cloned.1.call-start = ((), (), s32[]{:S(2)}) async-start(), calls=%async_computation.1 | async-start | bytes 2228224 | tf_op jit(solution)/shard_map/all_gather | solution.py:10
  7.3 97.7 %all-gather.5.cloned.1.call-start = ((), (), s32[]{:S(2)}) async-start(), calls=%async_computation.2 | async-start | bytes 4456448 | tf_op jit(solution)/shard_map/all_gather | solution.py:15
Sparse Core Ops, SparseCore 0:
  9.5 44.1 all-gather.2
  55.9 49.0 all-gather.4
where the time goes:
time: 133 us
  waiting for transfers between devices  98.4 us (74%)
  between operations  13.4 us (10%)
  blocking collectives  13.1 us (10%)
  matrix products  8.13 us (6%)
    all_gather x1, waiting for transfers between devices, shards(): whole_basis = lax.all_gather(basis, 'row', axis=0, tiled=True)  51.3 us
    all_gather x1, waiting for transfers between devices, shards(): lax.all_gather(orbitals, 'row', axis=0, tiled=True)  45.7 us
    all_to_all x1, blocking collectives, shards(): lax.all_to_all(applied, 'row', split_axis=1, concat_axis=0, tiled=True)  13.1 us
    dot_general x1, matrix products, shards(): jnp.dot(weighted, whole_basis, preferred_element_type=jnp.float32)  4.39 us
    dot_general x1, matrix products, shards(): lax.dot_general(whole_basis, received, (((0,), (0,)), ((), ())), preferre...  3.73 us
  transfers between devices with their start and end apart: 2, of which 2 were waited for; matrix products, arithmetic and copies ran while one was open for 0% of the time, Pallas kernels for 0%

commit v1 on v0

--- a/solution.py
+++ b/solution.py
@@ -2,9 +2,31 @@
 import jax.numpy as jnp
 from jax import lax
 from jax.sharding import PartitionSpec as P
+from jax.lax import axis_index, axis_size, ppermute
 
 
 def shards(orbitals, basis, kernel):
+
+    def tracks_compute(q_in):
+        outer, r_now = (axis_size("row"), axis_index("row"))
+        top = q_in.shape[1] // outer
+        low = list(q_in.shape)
+        low[1] = top
+        kept_arr = low[0]
+        low[0] = kept_arr * outer
+        reached = jnp.zeros(low, q_in.dtype)
+        for u in range(outer):
+            arr_out = lax.dynamic_slice_in_dim(q_in, (r_now ^ u) * top, top, axis=1)
+            if u:
+                buffers = []
+                for jj in range(outer):
+                    buffers.append((jj, jj ^ u))
+                arr_out = ppermute(arr_out, "row", buffers)
+            reached = lax.dynamic_update_slice_in_dim(
+                reached, arr_out, (r_now ^ u) * kept_arr, axis=0
+            )
+        return reached
+
     density = lax.dot_general(
         orbitals,
         lax.all_gather(orbitals, "row", axis=0, tiled=True),
@@ -16,7 +38,7 @@
     applied = jnp.dot(weighted, whole_basis, preferred_element_type=jnp.float32).astype(
         jnp.bfloat16
     )
-    received = lax.all_to_all(applied, "row", split_axis=1, concat_axis=0, tiled=True)
+    received = tracks_compute(applied)
     exchange_matrix = lax.dot_general(
         whole_basis, received, (((0,), (0,)), ((), ())), preferred_element_type=jnp.float32
     )

time: 133 us -> 146 us (1.098)
  starting transfers between devices: 0.04 us -> 21.1 us
  blocking collectives: 13.1 us -> 0 us
  waiting for transfers between devices: 98.4 us -> 102 us
    ppermute x0 -> x15, starting transfers between devices: none -> 21.1 us  [tracks_compute(): arr_out = ppermute(arr_out, 'row', buffers)]
    all_to_all x1 -> x0, blocking collectives: 13.1 us -> none  [shards(): lax.all_to_all(applied, 'row', split_axis=1, concat_axis=0, tiled=True)]
    ppermute x0 -> x15, waiting for transfers between devices: none -> 3.9 us  [tracks_compute(): arr_out = ppermute(arr_out, 'row', buffers)]
  transfers between devices with their start and end apart: 2 -> 17, of which waited for: 2 -> 4; matrix products, arithmetic and copies ran while one was open for 0% -> 0% of each run, Pallas kernels for 0% -> 0%
where the time goes in v1:
time: 146 us
  waiting for transfers between devices  102 us (70%)
  starting transfers between devices  21.1 us (14%)
  between operations  13.6 us (9%)
  matrix products  8.15 us (6%)
    all_gather x1, waiting for transfers between devices, shards(): whole_basis = lax.all_gather(basis, 'row', axis=0, tiled=True)  51.3 us
    all_gather x1, waiting for transfers between devices, shards(): lax.all_gather(orbitals, 'row', axis=0, tiled=True)  45.6 us
    ppermute x15, starting transfers between devices, tracks_compute(): arr_out = ppermute(arr_out, 'row', buffers)  21.1 us
    dot_general x1, matrix products, shards(): jnp.dot(weighted, whole_basis, preferred_element_type=jnp.float32)  4.39 us
    ppermute x15, waiting for transfers between devices, tracks_compute(): arr_out = ppermute(arr_out, 'row', buffers)  3.9 us
    dot_general x1, matrix products, shards(): lax.dot_general(whole_basis, received, (((0,), (0,)), ((), ())), preferre...  3.76 us
  transfers between devices with their start and end apart: 17, of which 4 were waited for; matrix products, arithmetic and copies ran while one was open for 0% of the time, Pallas kernels for 0%

profile of v1, /device:TPU:0, one launch (start us, length us, event | category | flops | bytes accessed | tf_op | source)
XLA Modules:
  0.0 145.6 jit_solution(16061802133155719486)
XLA Ops:
  6.5 0.7 all-gather.3.cloned.1.call-update
  7.3 0.7 all-gather.5.cloned.1.call-update
  8.1 45.6 %all-gather.3.cloned.1.call-done = bf16[2048,512]{1,0:T(8,128)(2,1)} async-done(((bf16[128,512]{1,0:T(8,128)(2,1)}), bf16[2048,512]{1,0:T(8,128)(2,1)}) %all-gather.3.cloned.1.call-update) | async-done | bytes 2097168 | tf_op jit(solution)/shard_map/all_gather | solution.py:32
  53.7 51.3 %all-gather.5.cloned.1.call-done = bf16[2048,1024]{1,0:T(8,128)(2,1)} async-done(((bf16[128,1024]{1,0:T(8,128)(2,1)}), bf16[2048,1024]{1,0:T(8,128)(2,1)}) %all-gather.5.cloned.1.call-update) | async-done | bytes 4194320 | tf_op jit(solution)/shard_map/all_gather | solution.py:37
  105.0 4.4 %convolution_convert_fusion = bf16[128,1024]{1,0:T(8,128)(2,1)S(1)} fusion(bf16[2048,1024]{1,0:T(8,128)(2,1)} %all-gather.5.cloned.1.call-done, bf16[128,512]{1,0:T(8,128)(2,1)} %param.3, bf16[2048,512]{1,0:T(8,128)(2,1)} %all-gather.3.cloned.1.call-done, bf16[128,2048]{1,0:T(8,128)(2,1)} %param.5), kind=kOutput, calls=%fused_computation.2 | convolution fusion | flops 806223872 | bytes 7208960 | tf_op jit(solution)/shard_map/dot_general | solution.py:38
  109.5 0.3 constant_dynamic-slice_fusion
  109.8 0.3 collective-permute-start
  110.1 0.6 collective-permute-start.1
  110.7 1.1 collective-permute-start.2
  111.8 1.5 %collective-permute-start.3 = (bf16[128,64]{1,0:T(8,128)(2,1)S(1)}, bf16[128,64]{1,0:T(8,128)(2,1)S(1)}, u32[]{:S(2)}, u32[]{:S(2)}) collective-permute-start(bf16[128,64]{1,0:T(8,128)(2,1)S(1)} %get-tuple-element.16), channel_id=1, source_target_pairs={{0,4},{1,5},{2,6},{3,7},{4,0},{5,1},{6,2},{7,3},{8,12},{9,13},{10,... | collective-permute-start | bytes 49160 | tf_op jit(solution)/shard_map/ppermute | solution.py:24
  113.3 0.3 collective-permute-start.4
  113.6 1.5 %collective-permute-start.5 = (bf16[128,64]{1,0:T(8,128)(2,1)S(1)}, bf16[128,64]{1,0:T(8,128)(2,1)S(1)}, u32[]{:S(2)}, u32[]{:S(2)}) collective-permute-start(bf16[128,64]{1,0:T(8,128)(2,1)S(1)} %get-tuple-element.14), channel_id=1, source_target_pairs={{0,6},{1,7},{2,4},{3,5},{4,2},{5,3},{6,0},{7,1},{8,14},{9,15},{10,... | collective-permute-start | bytes 49160 | tf_op jit(solution)/shard_map/ppermute | solution.py:24
  115.2 1.0 collective-permute-start.6
  116.2 1.9 %collective-permute-start.7 = (bf16[128,64]{1,0:T(8,128)(2,1)S(1)}, bf16[128,64]{1,0:T(8,128)(2,1)S(1)}, u32[]{:S(2)}, u32[]{:S(2)}) collective-permute-start(bf16[128,64]{1,0:T(8,128)(2,1)S(1)} %get-tuple-element.12), channel_id=1, source_target_pairs={{0,8},{1,9},{2,10},{3,11},{4,12},{5,13},{6,14},{7,15},{8,0},{9,1},... | collective-permute-start | bytes 49160 | tf_op jit(solution)/shard_map/ppermute | solution.py:24
  118.2 1.0 collective-permute-start.8
  119.2 1.9 %collective-permute-start.9 = (bf16[128,64]{1,0:T(8,128)(2,1)S(1)}, bf16[128,64]{1,0:T(8,128)(2,1)S(1)}, u32[]{:S(2)}, u32[]{:S(2)}) collective-permute-start(bf16[128,64]{1,0:T(8,128)(2,1)S(1)} %get-tuple-element.10), channel_id=1, source_target_pairs={{0,10},{1,11},{2,8},{3,9},{4,14},{5,15},{6,12},{7,13},{8,2},{9,3},... | collective-permute-start | bytes 49160 | tf_op jit(solution)/shard_map/ppermute | solution.py:24
  121.1 1.6 %collective-permute-start.10 = (bf16[128,64]{1,0:T(8,128)(2,1)S(1)}, bf16[128,64]{1,0:T(8,128)(2,1)S(1)}, u32[]{:S(2)}, u32[]{:S(2)}) collective-permute-start(bf16[128,64]{1,0:T(8,128)(2,1)S(1)} %get-tuple-element.9), channel_id=1, source_target_pairs={{0,11},{1,10},{2,9},{3,8},{4,15},{5,14},{6,13},{7,12},{8,3},{9,2},... | collective-permute-start | bytes 49160 | tf_op jit(solution)/shard_map/ppermute | solution.py:24
  122.7 1.9 %collective-permute-start.11 = (bf16[128,64]{1,0:T(8,128)(2,1)S(1)}, bf16[128,64]{1,0:T(8,128)(2,1)S(1)}, u32[]{:S(2)}, u32[]{:S(2)}) collective-permute-start(bf16[128,64]{1,0:T(8,128)(2,1)S(1)} %get-tuple-element.8), channel_id=1, source_target_pairs={{0,12},{1,13},{2,14},{3,15},{4,8},{5,9},{6,10},{7,11},{8,4},{9,5},... | collective-permute-start | bytes 49160 | tf_op jit(solution)/shard_map/ppermute | solution.py:24
  124.7 1.9 %collective-permute-start.12 = (bf16[128,64]{1,0:T(8,128)(2,1)S(1)}, bf16[128,64]{1,0:T(8,128)(2,1)S(1)}, u32[]{:S(2)}, u32[]{:S(2)}) collective-permute-start(bf16[128,64]{1,0:T(8,128)(2,1)S(1)} %get-tuple-element.7), channel_id=1, source_target_pairs={{0,13},{1,12},{2,15},{3,14},{4,9},{5,8},{6,11},{7,10},{8,5},{9,4},... | collective-permute-start | bytes 49160 | tf_op jit(solution)/shard_map/ppermute | solution.py:24
  126.6 2.0 %collective-permute-start.13 = (bf16[128,64]{1,0:T(8,128)(2,1)S(1)}, bf16[128,64]{1,0:T(8,128)(2,1)S(1)}, u32[]{:S(2)}, u32[]{:S(2)}) collective-permute-start(bf16[128,64]{1,0:T(8,128)(2,1)S(1)} %get-tuple-element.6), channel_id=1, source_target_pairs={{0,14},{1,15},{2,12},{3,13},{4,10},{5,11},{6,8},{7,9},{8,6},{9,7},... | collective-permute-start | bytes 49160 | tf_op jit(solution)/shard_map/ppermute | solution.py:24
  128.6 2.4 %collective-permute-start.14 = (bf16[128,64]{1,0:T(8,128)(2,1)S(1)}, bf16[128,64]{1,0:T(8,128)(2,1)S(1)}, u32[]{:S(2)}, u32[]{:S(2)}) collective-permute-start(bf16[128,64]{1,0:T(8,128)(2,1)S(1)} %get-tuple-element.5), channel_id=1, source_target_pairs={{0,15},{1,14},{2,13},{3,12},{4,11},{5,10},{6,9},{7,8},{8,7},{9,6},... | collective-permute-start | bytes 49160 | tf_op jit(solution)/shard_map/ppermute | solution.py:24
  131.1 2.1 %collective-permute-done.13 = bf16[128,64]{1,0:T(8,128)(2,1)S(1)} collective-permute-done((bf16[128,64]{1,0:T(8,128)(2,1)S(1)}, bf16[128,64]{1,0:T(8,128)(2,1)S(1)}, u32[]{:S(2)}, u32[]{:S(2)}) %collective-permute-start.13) | collective-permute-done | bytes 16416 | tf_op jit(solution)/shard_map/ppermute | solution.py:24
  133.3 1.7 %collective-permute-done.14 = bf16[128,64]{1,0:T(8,128)(2,1)S(1)} collective-permute-done((bf16[128,64]{1,0:T(8,128)(2,1)S(1)}, bf16[128,64]{1,0:T(8,128)(2,1)S(1)}, u32[]{:S(2)}, u32[]{:S(2)}) %collective-permute-start.14) | collective-permute-done | bytes 16416 | tf_op jit(solution)/shard_map/ppermute | solution.py:24
  135.0 3.8 %convolution_bitcast_fusion = f32[1024,64]{0,1:T(8,128)} fusion(bf16[2048,64]{1,0:T(8,128)(2,1)S(1)} %constant_dynamic-update-slice_fusion.14, bf16[2048,1024]{1,0:T(8,128)(2,1)} %all-gather.5.cloned.1.call-done), kind=kOutput, calls=%fused_computation.3 | convolution fusion | flops 268435456 | bytes 4718592 | tf_op jit(solution)/shard_map/dot_general | solution.py:42
  (31 shorter events, 0.3 us)
Async XLA Ops:
  6.5 47.2 %all-gather.3.cloned.1.call-start = ((), (), s32[]{:S(2)}) async-start(), calls=%async_computation | async-start | bytes 2228224 | tf_op jit(solution)/shard_map/all_gather | solution.py:32
  7.3 97.7 %all-gather.5.cloned.1.call-start = ((), (), s32[]{:S(2)}) async-start(), calls=%async_computation.1 | async-start | bytes 4456448 | tf_op jit(solution)/shard_map/all_gather | solution.py:37
  109.8 3.8 %collective-permute-start = (bf16[128,64]{1,0:T(8,128)(2,1)S(1)}, bf16[128,64]{1,0:T(8,128)(2,1)S(1)}, u32[]{:S(2)}, u32[]{:S(2)}) collective-permute-start(bf16[128,64]{1,0:T(8,128)(2,1)S(1)} %get-tuple-element.19), channel_id=1, source_target_pairs={{0,1},{1,0},{2,3},{3,2},{4,5},{5,4},{6,7},{7,6},{8,9},{9,8},{10,11... | collective-permute-start | bytes 49160 | tf_op jit(solution)/shard_map/ppermute | solution.py:24
  110.1 5.0 %collective-permute-start.1 = (bf16[128,64]{1,0:T(8,128)(2,1)S(1)}, bf16[128,64]{1,0:T(8,128)(2,1)S(1)}, u32[]{:S(2)}, u32[]{:S(2)}) collective-permute-start(bf16[128,64]{1,0:T(8,128)(2,1)S(1)} %get-tuple-element.18), channel_id=1, source_target_pairs={{0,2},{1,3},{2,0},{3,1},{4,6},{5,7},{6,4},{7,5},{8,10},{9,11},{10,... | collective-permute-start | bytes 49160 | tf_op jit(solution)/shard_map/ppermute | solution.py:24
  110.7 5.5 %collective-permute-start.2 = (bf16[128,64]{1,0:T(8,128)(2,1)S(1)}, bf16[128,64]{1,0:T(8,128)(2,1)S(1)}, u32[]{:S(2)}, u32[]{:S(2)}) collective-permute-start(bf16[128,64]{1,0:T(8,128)(2,1)S(1)} %get-tuple-element.17), channel_id=1, source_target_pairs={{0,3},{1,2},{2,1},{3,0},{4,7},{5,6},{6,5},{7,4},{8,11},{9,10},{10,... | collective-permute-start | bytes 49160 | tf_op jit(solution)/shard_map/ppermute | solution.py:24
  111.8 6.4 %collective-permute-start.3 = (bf16[128,64]{1,0:T(8,128)(2,1)S(1)}, bf16[128,64]{1,0:T(8,128)(2,1)S(1)}, u32[]{:S(2)}, u32[]{:S(2)}) collective-permute-start(bf16[128,64]{1,0:T(8,128)(2,1)S(1)} %get-tuple-element.16), channel_id=1, source_target_pairs={{0,4},{1,5},{2,6},{3,7},{4,0},{5,1},{6,2},{7,3},{8,12},{9,13},{10,... | collective-permute-start | bytes 49160 | tf_op jit(solution)/shard_map/ppermute | solution.py:24
  113.3 5.9 %collective-permute-start.4 = (bf16[128,64]{1,0:T(8,128)(2,1)S(1)}, bf16[128,64]{1,0:T(8,128)(2,1)S(1)}, u32[]{:S(2)}, u32[]{:S(2)}) collective-permute-start(bf16[128,64]{1,0:T(8,128)(2,1)S(1)} %get-tuple-element.15), channel_id=1, source_target_pairs={{0,5},{1,4},{2,7},{3,6},{4,1},{5,0},{6,3},{7,2},{8,13},{9,12},{10,... | collective-permute-start | bytes 49160 | tf_op jit(solution)/shard_map/ppermute | solution.py:24
  113.6 7.5 %collective-permute-start.5 = (bf16[128,64]{1,0:T(8,128)(2,1)S(1)}, bf16[128,64]{1,0:T(8,128)(2,1)S(1)}, u32[]{:S(2)}, u32[]{:S(2)}) collective-permute-start(bf16[128,64]{1,0:T(8,128)(2,1)S(1)} %get-tuple-element.14), channel_id=1, source_target_pairs={{0,6},{1,7},{2,4},{3,5},{4,2},{5,3},{6,0},{7,1},{8,14},{9,15},{10,... | collective-permute-start | bytes 49160 | tf_op jit(solution)/shard_map/ppermute | solution.py:24
  115.2 7.6 %collective-permute-start.6 = (bf16[128,64]{1,0:T(8,128)(2,1)S(1)}, bf16[128,64]{1,0:T(8,128)(2,1)S(1)}, u32[]{:S(2)}, u32[]{:S(2)}) collective-permute-start(bf16[128,64]{1,0:T(8,128)(2,1)S(1)} %get-tuple-element.13), channel_id=1, source_target_pairs={{0,7},{1,6},{2,5},{3,4},{4,3},{5,2},{6,1},{7,0},{8,15},{9,14},{10,... | collective-permute-start | bytes 49160 | tf_op jit(solution)/shard_map/ppermute | solution.py:24
  116.2 8.4 %collective-permute-start.7 = (bf16[128,64]{1,0:T(8,128)(2,1)S(1)}, bf16[128,64]{1,0:T(8,128)(2,1)S(1)}, u32[]{:S(2)}, u32[]{:S(2)}) collective-permute-start(bf16[128,64]{1,0:T(8,128)(2,1)S(1)} %get-tuple-element.12), channel_id=1, source_target_pairs={{0,8},{1,9},{2,10},{3,11},{4,12},{5,13},{6,14},{7,15},{8,0},{9,1},... | collective-permute-start | bytes 49160 | tf_op jit(solution)/shard_map/ppermute | solution.py:24
  118.2 8.4 %collective-permute-start.8 = (bf16[128,64]{1,0:T(8,128)(2,1)S(1)}, bf16[128,64]{1,0:T(8,128)(2,1)S(1)}, u32[]{:S(2)}, u32[]{:S(2)}) collective-permute-start(bf16[128,64]{1,0:T(8,128)(2,1)S(1)} %get-tuple-element.11), channel_id=1, source_target_pairs={{0,9},{1,8},{2,11},{3,10},{4,13},{5,12},{6,15},{7,14},{8,1},{9,0},... | collective-permute-start | bytes 49160 | tf_op jit(solution)/shard_map/ppermute | solution.py:24
  119.2 9.4 %collective-permute-start.9 = (bf16[128,64]{1,0:T(8,128)(2,1)S(1)}, bf16[128,64]{1,0:T(8,128)(2,1)S(1)}, u32[]{:S(2)}, u32[]{:S(2)}) collective-permute-start(bf16[128,64]{1,0:T(8,128)(2,1)S(1)} %get-tuple-element.10), channel_id=1, source_target_pairs={{0,10},{1,11},{2,8},{3,9},{4,14},{5,15},{6,12},{7,13},{8,2},{9,3},... | collective-permute-start | bytes 49160 | tf_op jit(solution)/shard_map/ppermute | solution.py:24
  121.1 9.9 %collective-permute-start.10 = (bf16[128,64]{1,0:T(8,128)(2,1)S(1)}, bf16[128,64]{1,0:T(8,128)(2,1)S(1)}, u32[]{:S(2)}, u32[]{:S(2)}) collective-permute-start(bf16[128,64]{1,0:T(8,128)(2,1)S(1)} %get-tuple-element.9), channel_id=1, source_target_pairs={{0,11},{1,10},{2,9},{3,8},{4,15},{5,14},{6,13},{7,12},{8,3},{9,2},... | collective-permute-start | bytes 49160 | tf_op jit(solution)/shard_map/ppermute | solution.py:24
  122.7 8.3 %collective-permute-start.11 = (bf16[128,64]{1,0:T(8,128)(2,1)S(1)}, bf16[128,64]{1,0:T(8,128)(2,1)S(1)}, u32[]{:S(2)}, u32[]{:S(2)}) collective-permute-start(bf16[128,64]{1,0:T(8,128)(2,1)S(1)} %get-tuple-element.8), channel_id=1, source_target_pairs={{0,12},{1,13},{2,14},{3,15},{4,8},{5,9},{6,10},{7,11},{8,4},{9,5},... | collective-permute-start | bytes 49160 | tf_op jit(solution)/shard_map/ppermute | solution.py:24
  124.7 6.4 %collective-permute-start.12 = (bf16[128,64]{1,0:T(8,128)(2,1)S(1)}, bf16[128,64]{1,0:T(8,128)(2,1)S(1)}, u32[]{:S(2)}, u32[]{:S(2)}) collective-permute-start(bf16[128,64]{1,0:T(8,128)(2,1)S(1)} %get-tuple-element.7), channel_id=1, source_target_pairs={{0,13},{1,12},{2,15},{3,14},{4,9},{5,8},{6,11},{7,10},{8,5},{9,4},... | collective-permute-start | bytes 49160 | tf_op jit(solution)/shard_map/ppermute | solution.py:24
  126.6 6.7 %collective-permute-start.13 = (bf16[128,64]{1,0:T(8,128)(2,1)S(1)}, bf16[128,64]{1,0:T(8,128)(2,1)S(1)}, u32[]{:S(2)}, u32[]{:S(2)}) collective-permute-start(bf16[128,64]{1,0:T(8,128)(2,1)S(1)} %get-tuple-element.6), channel_id=1, source_target_pairs={{0,14},{1,15},{2,12},{3,13},{4,10},{5,11},{6,8},{7,9},{8,6},{9,7},... | collective-permute-start | bytes 49160 | tf_op jit(solution)/shard_map/ppermute | solution.py:24
  128.6 6.4 %collective-permute-start.14 = (bf16[128,64]{1,0:T(8,128)(2,1)S(1)}, bf16[128,64]{1,0:T(8,128)(2,1)S(1)}, u32[]{:S(2)}, u32[]{:S(2)}) collective-permute-start(bf16[128,64]{1,0:T(8,128)(2,1)S(1)} %get-tuple-element.5), channel_id=1, source_target_pairs={{0,15},{1,14},{2,13},{3,12},{4,11},{5,10},{6,9},{7,8},{8,7},{9,6},... | collective-permute-start | bytes 49160 | tf_op jit(solution)/shard_map/ppermute | solution.py:24
Sparse Core Ops, SparseCore 0:
  9.5 44.1 all-gather.2
  55.9 49.0 all-gather.4
